TPU v7x, 128 devices: a whole 4x4x4 slice. The times are simulated.
128 devices in a mesh: row: 8 (over y_hi, z), col: 16 (over y_lo, x, core).
Axes of the slice: x: 4, y: 4 (y_hi: 2, y_lo: 2; y = y_hi * 2 + y_lo), z: 4, core: 2. Of those that a mesh axis runs over, the one named last changes fastest.
Arguments:
- covariance: float32 [16384, 16384], P('row', 'col'), may hold values from -6 to 6
- wind_direction: int32 [2, 16384], replicated, may hold values from 0 to 3
- wind_speed: int32 [2, 16384], replicated, may hold values from 0 to 7
- speed_table: float32 [2, 8], replicated, may hold values from 0.05 to 0.4
- diffusivity: float32 [128], replicated, may hold values from 0.005 to 0.05
Outputs:
- predicted_covariance: float32 [16384, 16384], P('row', 'col')
All inputs are finite; a program needn't handle non-finite values.
Results may differ from a plain program's by a relative error of at most 0.00002.
Values sent between devices are 32-bit elements; how exact they have to be, the bound alone decides.
A program may use at most 192 MiB of HBM per device.

v0:
```python
import jax
import jax.numpy as jnp
from jax import lax
from jax.sharding import PartitionSpec as P

NLAT = 128
NLON = 128
SUBSTEPS = 2


def extended(array, sides, width):
    for axis, dim in sides:
        count, length = (lax.axis_size(axis), array.shape[dim])
        up = [(i, (i + 1) % count) for i in range(count - 1)]
        down = [(j, i) for i, j in up]
        last = lax.slice_in_dim(array, length - width, length, axis=dim)
        first = lax.slice_in_dim(array, 0, width, axis=dim)
        before = lax.ppermute(last, axis, up)
        after = lax.ppermute(first, axis, down)
        array = jnp.concatenate([before, array, after], axis=dim)
    return array


def build_coefficients(wind_direction, wind_speed, speed_table, diffusivity, nlat, nlon):
    substeps = wind_direction.shape[0]
    category_list = speed_table.shape[1]
    onehot = (wind_speed[:, :, None] == jnp.arange(category_list, dtype=jnp.int32)).astype(
        speed_table.dtype
    )
    lon_courant = jnp.sum(onehot * speed_table[0], axis=2).reshape(substeps, nlat, nlon)
    lat_courant = jnp.sum(onehot * speed_table[1], axis=2).reshape(substeps, nlat, nlon)
    eastward = (wind_direction % 2 == 0).astype(speed_table.dtype).reshape(substeps, nlat, nlon)
    northward = (wind_direction // 2 == 0).astype(speed_table.dtype).reshape(substeps, nlat, nlon)
    diffusion = diffusivity[None, :, None]
    center = 1.0 - lon_courant - lat_courant - 4.0 * diffusion
    western = lon_courant * eastward + diffusion
    eastern = lon_courant * (1.0 - eastward) + diffusion
    southern = lat_courant * northward + diffusion
    northern = lat_courant * (1.0 - northward) + diffusion
    return jnp.stack([center, western, eastern, southern, northern], axis=1)


def substep(tracer, weights):
    span_length = tracer.shape[0]
    middle = tracer[1 : span_length - 1]
    southern = tracer[0 : span_length - 2]
    northern = tracer[2:span_length]
    return (
        weights[0] * middle
        + weights[1] * jnp.roll(middle, 1, axis=1)
        + weights[2] * jnp.roll(middle, -1, axis=1)
        + weights[3] * southern
        + weights[4] * northern
    )


def advance_rows(padded, table_padded, lat_start, lat_count):
    substeps = table_padded.shape[0]
    tracer = padded
    for section_idx in range(substeps):
        span_length = lat_count + 2 * (substeps - 1 - section_idx)
        weights = lax.dynamic_slice_in_dim(
            table_padded[section_idx], lat_start + section_idx + 1, span_length, 1
        )
        tracer = substep(tracer, weights[..., None])
    return tracer


def advance_flat(padded, table_padded, lat_start, lat_count, nlon):
    substeps = table_padded.shape[0]
    tracer = padded
    for section_idx in range(substeps):
        span_length = lat_count + 2 * (substeps - 1 - section_idx)
        weights = lax.dynamic_slice_in_dim(
            table_padded[section_idx], lat_start + section_idx + 1, span_length, 1
        )
        weights = weights.reshape(weights.shape[0], 1, span_length * nlon)
        total = tracer.shape[1]
        middle = tracer[:, nlon : total - nlon]
        southern = tracer[:, 0 : total - 2 * nlon]
        northern = tracer[:, 2 * nlon : total]
        longitude = (jnp.arange(span_length * nlon, dtype=jnp.int32) % nlon)[None, :]
        western = jnp.where(
            longitude == 0, jnp.roll(middle, 1 - nlon, axis=1), jnp.roll(middle, 1, axis=1)
        )
        eastern = jnp.where(
            longitude == nlon - 1, jnp.roll(middle, nlon - 1, axis=1), jnp.roll(middle, -1, axis=1)
        )
        tracer = (
            weights[0] * middle
            + weights[1] * western
            + weights[2] * eastern
            + weights[3] * southern
            + weights[4] * northern
        )
    return tracer


def local(covariance, wind_direction, wind_speed, speed_table, diffusivity):
    weight_table = build_coefficients(
        wind_direction, wind_speed, speed_table, diffusivity, NLAT, NLON
    )
    table_padded = jnp.pad(weight_table, ((0, 0), (0, 0), (SUBSTEPS, SUBSTEPS), (0, 0)))
    rows_tile, cols_tile = covariance.shape
    lat_rows = rows_tile // NLON
    lat_start = lax.axis_index("row") * lat_rows
    tracer = covariance.reshape(lat_rows, NLON, cols_tile)
    padded = extended(tracer, (("row", 0),), SUBSTEPS)
    advected = advance_rows(padded, table_padded, lat_start, lat_rows).reshape(rows_tile, cols_tile)
    latitude_columns = cols_tile // NLON
    column_offset = lax.axis_index("col") * latitude_columns
    column_padded = extended(advected, (("col", 1),), SUBSTEPS * NLON)
    predicted_covariance = advance_flat(
        column_padded, table_padded, column_offset, latitude_columns, NLON
    )
    return predicted_covariance


def solution(mesh):
    return jax.shard_map(
        local,
        mesh=mesh,
        in_specs=(P("row", "col"), P(), P(), P(), P()),
        out_specs=P("row", "col"),
        check_vma=False,
    )
```

profile of v0, /device:TPU:23, one launch (start us, length us, event | category | flops | bytes accessed | tf_op | source)
XLA Modules:
  0.0 244.0 jit_solution(3011217883250172866)
XLA Ops:
  0.0 2.7 %fusion.59 = (f32[256,1024]{1,0:T(8,128)S(1)}, f32[256,1024]{1,0:T(8,128)}) fusion(f32[2048,1024]{1,0:T(8,128)} %param.5), kind=kLoop, calls=%fused_computation.130 | loop fusion | bytes 4194304 | tf_op jit(solution)/shard_map/slice | solution.py:16
  2.7 5.4 %collective-permute-start.1 = (f32[2,128,1024]{2,1,0:T(8,128)}, f32[2,128,1024]{2,1,0:T(8,128)S(1)}, u32[]{:S(2)}, u32[]{:S(2)}) collective-permute-start(f32[2,128,1024]{2,1,0:T(8,128)} %bitcast.8), channel_id=1, source_target_pairs={{16,0},{32,16},{48,32},{64,48},{80,64},{96,80},{112,96},{17,1},{33... | collective-permute-start | bytes 3145736 | tf_op jit(solution)/shard_map/ppermute | solution.py:19
  8.1 1.9 collective-permute-start
  11.5 1.5 compare_bitcast_fusion
  13.0 1.7 select_reduce_fusion.1
  18.6 11.7 %collective-permute-done.1 = f32[2,128,1024]{2,1,0:T(8,128)S(1)} collective-permute-done((f32[2,128,1024]{2,1,0:T(8,128)}, f32[2,128,1024]{2,1,0:T(8,128)S(1)}, u32[]{:S(2)}, u32[]{:S(2)}) %collective-permute-start.1) | collective-permute-done | bytes 1048608 | tf_op jit(solution)/shard_map/ppermute | solution.py:19
  30.3 7.1 %collective-permute-done = f32[2,128,1024]{2,1,0:T(8,128)S(1)} collective-permute-done((f32[2,128,1024]{2,1,0:T(8,128)S(1)}, f32[2,128,1024]{2,1,0:T(8,128)S(1)}, u32[]{:S(2)}, u32[]{:S(2)}) %collective-permute-start) | collective-permute-done | bytes 1048608 | tf_op jit(solution)/shard_map/ppermute | solution.py:18
  37.4 9.4 %pad_maximum_fusion.1 = f32[20,128,1024]{2,1,0:T(8,128)} fusion(f32[2,128,1024]{2,1,0:T(8,128)S(1)} %collective-permute-done.1, f32[16,128,1024]{2,1,0:T(8,128)} %bitcast.105, f32[2,128,1024]{2,1,0:T(8,128)S(1)} %collective-permute-done), kind=kLoop, calls=%fused_computation.6 | loop fusion | flops 5242880 | bytes 20971520 | tf_op jit(solution)/shard_map/concatenate | solution.py:20
  46.8 15.0 %fusion.55 = (f32[18,127,1024]{2,1,0:T(8,128)}, f32[18,127,1024]{2,1,0:T(8,128)}) fusion(f32[20,128,1024]{2,1,0:T(8,128)} %pad_maximum_fusion.1), kind=kLoop, calls=%fused_computation.126 | loop fusion | bytes 37453824 | tf_op jit(solution)/shard_map/jit(_roll_static)/slice | solution.py:51
  61.8 20.1 %fusion.10 = f32[18,128,1024]{2,1,0:T(8,128)} fusion(f32[2,128,1024]{2,1,0:T(8,128)S(1)} %collective-permute-done.1, f32[16,128,1024]{2,1,0:T(8,128)} %bitcast.106, f32[2,128,1024]{2,1,0:T(8,128)S(1)} %collective-permute-done, f32[20,128,1024]{2,1,0:T(8,128)} %pad_maximum_fusion.1, f32[18,127,1024]{2,1,0:T(8,128)} %get-tuple-element.20, ...), kind=kLoop, calls=%fused_computation.18 | loop fusion | flops 40108032 | bytes 48133120 | tf_op jit(solution)/shard_map/add | solution.py:49
  81.8 1.4 fusion.57
  83.3 13.9 %fusion.56 = (f32[16,127,1024]{2,1,0:T(8,128)}, f32[16,127,1024]{2,1,0:T(8,128)}) fusion(f32[18,128,1024]{2,1,0:T(8,128)} %fusion.10), kind=kLoop, calls=%fused_computation.127 | loop fusion | bytes 33292288 | tf_op jit(solution)/shard_map/jit(_roll_static)/slice | solution.py:51
  97.3 8.0 %fusion.18 = f32[16,128,1024]{2,1,0:T(8,128)S(1)} fusion(f32[18,128,1024]{2,1,0:T(8,128)S(1)} %bitcast.101, f32[16,127,1024]{2,1,0:T(8,128)} %get-tuple-element.22, f32[16,1,1024]{2,1,0:T(1,128)S(1)} %get-tuple-element.24, f32[16,1,1024]{2,1,0:T(1,128)S(1)} %get-tuple-element.23, f32[16,127,1024]{2,1,0:T(8,128)} %get-tuple-element.21, ...), kind=kLoop, calls=%fused_computation.36 | loop fusion | flops 23068672 | bytes 50372608 | tf_op jit(solution)/shard_map/add | solution.py:49
  105.3 3.4 %copy-done.1 = f32[16,128,1024]{2,1,0:T(8,128)} copy-done((f32[16,128,1024]{2,1,0:T(8,128)}, f32[16,128,1024]{2,1,0:T(8,128)S(1)}, u32[]{:S(2)}) %copy-start.1) | copy-done | bytes 8388632
  108.7 2.3 fusion.58
  111.0 5.5 %collective-permute-start.2 = (f32[2048,256]{1,0:T(8,128)}, f32[2048,256]{1,0:T(8,128)S(1)}, u32[]{:S(2)}, u32[]{:S(2)}) collective-permute-start(f32[2048,256]{1,0:T(8,128)} %get-tuple-element.25), channel_id=1, source_target_pairs={{0,1},{1,2},{2,3},{3,4},{4,5},{5,6},{6,7},{7,8},{8,9},{9,10},{10,1... | collective-permute-start | bytes 6291464 | tf_op jit(solution)/shard_map/ppermute | solution.py:18
  116.4 2.1 collective-permute-start.3
  119.4 20.3 %collective-permute-done.2 = f32[2048,256]{1,0:T(8,128)S(1)} collective-permute-done((f32[2048,256]{1,0:T(8,128)}, f32[2048,256]{1,0:T(8,128)S(1)}, u32[]{:S(2)}, u32[]{:S(2)}) %collective-permute-start.2) | collective-permute-done | bytes 2097184 | tf_op jit(solution)/shard_map/ppermute | solution.py:18
  139.7 6.5 %collective-permute-done.3 = f32[2048,256]{1,0:T(8,128)} collective-permute-done((f32[2048,256]{1,0:T(8,128)}, f32[2048,256]{1,0:T(8,128)}, u32[]{:S(2)}, u32[]{:S(2)}) %collective-permute-start.3) | collective-permute-done | bytes 2097184 | tf_op jit(solution)/shard_map/ppermute | solution.py:19
  146.2 5.3 %pad_maximum_fusion = f32[2048,1536]{1,0:T(8,128)S(1)} fusion(f32[2048,256]{1,0:T(8,128)} %collective-permute-done.3, f32[2048,1024]{1,0:T(8,128)} %bitcast.103, f32[2048,256]{1,0:T(8,128)S(1)} %collective-permute-done.2), kind=kLoop, calls=%fused_computation | loop fusion | flops 6291456 | bytes 25165824 | tf_op jit(solution)/shard_map/concatenate | solution.py:20
  151.6 9.3 %fusion.49 = (f32[2048,1279]{1,0:T(8,128)}, f32[2048,1279]{1,0:T(8,128)}) fusion(f32[2048,1536]{1,0:T(8,128)S(1)} %pad_maximum_fusion), kind=kLoop, calls=%fused_computation.120 | loop fusion | bytes 41910272 | tf_op jit(solution)/shard_map/jit(_roll_static)/slice | solution.py:87
  160.9 1.5 copy-done
  162.4 8.2 %fusion.50 = (f32[2048,1153]{1,0:T(8,128)}, f32[2048,1153]{1,0:T(8,128)}) fusion(f32[2048,1536]{1,0:T(8,128)S(1)} %pad_maximum_fusion), kind=kLoop, calls=%fused_computation.121 | loop fusion | bytes 37781504 | tf_op jit(solution)/shard_map/jit(_roll_static)/slice | solution.py:87
  170.8 1.6 slice.347
  172.3 1.6 slice.345
  173.9 29.9 %fusion.3 = f32[2048,1280]{1,0:T(8,128)} fusion(f32[2048,1536]{1,0:T(8,128)} %copy-done, f32[2048,127]{1,0:T(8,128)S(1)} %slice.344, f32[2048,1153]{1,0:T(8,128)} %get-tuple-element.10, f32[2048,1279]{1,0:T(8,128)} %get-tuple-element.8, f32[2048,1]{1,0:T(8,128)S(1)} %slice.345, f32[2048,1153]{1,0:T(8,128)} %get-tuple-element.9, f32[2048,127]{1,0:T(8,128)S(1)} %slice.347, ...), kind=kLoop, calls=%fused_computation.5 | loop fusion | flops 44564480 | bytes 75525632 | tf_op jit(solution)/shard_map/add | solution.py:90
  203.8 3.2 %fusion.52 = (f32[2048,1]{1,0:T(8,128)}, f32[2048,1]{1,0:T(8,128)}) fusion(f32[2048,1280]{1,0:T(8,128)} %fusion.3), kind=kLoop, calls=%fused_computation.123 | loop fusion | bytes 32768 | tf_op jit(solution)/shard_map/jit(_roll_static)/slice | solution.py:87
  207.1 3.4 %fusion.53 = (f32[2048,127]{1,0:T(8,128)}, f32[2048,127]{1,0:T(8,128)}) fusion(f32[2048,1280]{1,0:T(8,128)} %fusion.3), kind=kLoop, calls=%fused_computation.124 | loop fusion | bytes 4161536 | tf_op jit(solution)/shard_map/jit(_roll_static)/slice | solution.py:87
  210.5 10.0 %fusion.51 = (f32[2048,1023]{1,0:T(8,128)S(1)}, f32[2048,1023]{1,0:T(8,128)}) fusion(f32[2048,1280]{1,0:T(8,128)} %fusion.3), kind=kLoop, calls=%fused_computation.122 | loop fusion | bytes 33521664 | tf_op jit(solution)/shard_map/jit(_roll_static)/slice | solution.py:87
  220.5 0.8 slice-done.2
  221.3 7.4 %fusion.54 = (f32[2048,897]{1,0:T(8,128)}, f32[2048,897]{1,0:T(8,128)}) fusion(f32[2048,1280]{1,0:T(8,128)S(1)} %bitcast.99), kind=kLoop, calls=%fused_computation.125 | loop fusion | bytes 29392896 | tf_op jit(solution)/shard_map/jit(_roll_static)/slice | solution.py:87
  228.7 15.3 %fusion.14 = f32[2048,1024]{1,0:T(8,128)} fusion(f32[2048,1280]{1,0:T(8,128)S(1)} %bitcast.99, f32[2048,127]{1,0:T(8,128)} %get-tuple-element.16, f32[2048,897]{1,0:T(8,128)} %get-tuple-element.18, f32[2048,1023]{1,0:T(8,128)} %get-tuple-element.12, f32[2048,1]{1,0:T(8,128)} %get-tuple-element.14, f32[2048,897]{1,0:T(8,128)} %get-tuple-element.17, ...), kind=kLoop, calls=%fused_computation.29 | loop fusion | flops 31457280 | bytes 67131392 | tf_op jit(solution)/shard_map/add | solution.py:90
  (43 shorter events, 6.3 us)
Async XLA Ops:
  2.7 27.6 %collective-permute-start.1 = (f32[2,128,1024]{2,1,0:T(8,128)}, f32[2,128,1024]{2,1,0:T(8,128)S(1)}, u32[]{:S(2)}, u32[]{:S(2)}) collective-permute-start(f32[2,128,1024]{2,1,0:T(8,128)} %bitcast.8), channel_id=1, source_target_pairs={{16,0},{32,16},{48,32},{64,48},{80,64},{96,80},{112,96},{17,1},{33... | collective-permute-start | bytes 3145736 | tf_op jit(solution)/shard_map/ppermute | solution.py:19
  8.1 29.2 %collective-permute-start = (f32[2,128,1024]{2,1,0:T(8,128)S(1)}, f32[2,128,1024]{2,1,0:T(8,128)S(1)}, u32[]{:S(2)}, u32[]{:S(2)}) collective-permute-start(f32[2,128,1024]{2,1,0:T(8,128)S(1)} %bitcast.113), channel_id=1, source_target_pairs={{0,16},{16,32},{32,48},{48,64},{64,80},{80,96},{96,112},{1,17},{17... | collective-permute-start | bytes 3145736 | tf_op jit(solution)/shard_map/ppermute | solution.py:18
  17.9 19.5 %copy-start.2 = (f32[1,5,132,128]{3,2,0,1:T(8,128)}, f32[1,5,132,128]{3,2,0,1:T(8,128)S(1)}, u32[]{:S(2)}) copy-start(f32[1,5,132,128]{3,2,0,1:T(8,128)S(1)} %get-tuple-element.29) | copy-start | bytes 1013764
  81.8 15.4 %slice-start.3 = ((s8[9437184]{0:T(1024)(128)(4,1)}), s8[4194304]{0:T(1024)(128)(4,1)S(1)}, s32[]{:S(2)}) async-start(s8[9437184]{0:T(1024)(128)(4,1)} %bitcast.100), calls=%async_computation.3 | async-start | bytes 8388608
  83.3 13.9 %slice-start.4 = ((s8[9437184]{0:T(1024)(128)(4,1)}), s8[4194304]{0:T(1024)(128)(4,1)S(1)}, s32[]{:S(2)}) async-start(s8[9437184]{0:T(1024)(128)(4,1)} %bitcast.100), calls=%async_computation.4 | async-start | bytes 8388608
  83.3 13.9 %slice-start.5 = ((s8[9437184]{0:T(1024)(128)(4,1)}), s8[1048576]{0:T(1024)(128)(4,1)S(1)}, s32[]{:S(2)}) async-start(s8[9437184]{0:T(1024)(128)(4,1)} %bitcast.100), calls=%async_computation.5 | async-start | bytes 2097152
  83.3 13.9 %copy-start.3 = (f32[16,128]{1,0:T(8,128)S(1)}, f32[16,128]{1,0:T(8,128)}, u32[]{:S(2)}) copy-start(f32[16,128]{1,0:T(8,128)} %get-tuple-element.41) | copy-start | bytes 24580
  83.3 13.9 %copy-start.4 = (f32[16,128]{1,0:T(8,128)S(1)}, f32[16,128]{1,0:T(8,128)}, u32[]{:S(2)}) copy-start(f32[16,128]{1,0:T(8,128)} %get-tuple-element.42) | copy-start | bytes 24580
  83.3 13.9 %copy-start.5 = (f32[16,128]{1,0:T(8,128)S(1)}, f32[16,128]{1,0:T(8,128)}, u32[]{:S(2)}) copy-start(f32[16,128]{1,0:T(8,128)} %get-tuple-element.43) | copy-start | bytes 24580
  83.3 13.9 %copy-start.6 = (f32[16,128]{1,0:T(8,128)S(1)}, f32[16,128]{1,0:T(8,128)}, u32[]{:S(2)}) copy-start(f32[16,128]{1,0:T(8,128)} %get-tuple-element.44) | copy-start | bytes 24580
  83.3 13.9 %copy-start.7 = (f32[16,128]{1,0:T(8,128)S(1)}, f32[16,128]{1,0:T(8,128)}, u32[]{:S(2)}) copy-start(f32[16,128]{1,0:T(8,128)} %get-tuple-element.45) | copy-start | bytes 24580
  105.3 3.4 %copy-start.1 = (f32[16,128,1024]{2,1,0:T(8,128)}, f32[16,128,1024]{2,1,0:T(8,128)S(1)}, u32[]{:S(2)}) copy-start(f32[16,128,1024]{2,1,0:T(8,128)S(1)} %fusion.18) | copy-start | bytes 25165828
  111.0 28.7 %collective-permute-start.2 = (f32[2048,256]{1,0:T(8,128)}, f32[2048,256]{1,0:T(8,128)S(1)}, u32[]{:S(2)}, u32[]{:S(2)}) collective-permute-start(f32[2048,256]{1,0:T(8,128)} %get-tuple-element.25), channel_id=1, source_target_pairs={{0,1},{1,2},{2,3},{3,4},{4,5},{5,6},{6,7},{7,8},{8,9},{9,10},{10,1... | collective-permute-start | bytes 6291464 | tf_op jit(solution)/shard_map/ppermute | solution.py:18
  116.4 29.8 %collective-permute-start.3 = (f32[2048,256]{1,0:T(8,128)}, f32[2048,256]{1,0:T(8,128)}, u32[]{:S(2)}, u32[]{:S(2)}) collective-permute-start(f32[2048,256]{1,0:T(8,128)} %get-tuple-element.26), channel_id=1, source_target_pairs={{1,0},{2,1},{3,2},{4,3},{5,4},{6,5},{7,6},{8,7},{9,8},{10,9},{11,1... | collective-permute-start | bytes 6291464 | tf_op jit(solution)/shard_map/ppermute | solution.py:19
  151.6 10.8 %copy-start = (f32[2048,1536]{1,0:T(8,128)}, f32[2048,1536]{1,0:T(8,128)S(1)}, u32[]{:S(2)}) copy-start(f32[2048,1536]{1,0:T(8,128)S(1)} %pad_maximum_fusion) | copy-start | bytes 37748740
  207.1 13.5 %slice-start = ((s8[10485760]{0:T(1024)(128)(4,1)}), s8[4194304]{0:T(1024)(128)(4,1)S(1)}, s32[]{:S(2)}) async-start(s8[10485760]{0:T(1024)(128)(4,1)} %bitcast.98), calls=%async_computation | async-start | bytes 8388608
  210.5 10.0 %slice-start.1 = ((s8[10485760]{0:T(1024)(128)(4,1)}), s8[4194304]{0:T(1024)(128)(4,1)S(1)}, s32[]{:S(2)}) async-start(s8[10485760]{0:T(1024)(128)(4,1)} %bitcast.98), calls=%async_computation.1 | async-start | bytes 8388608
  210.5 10.8 %slice-start.2 = ((s8[10485760]{0:T(1024)(128)(4,1)}), s8[2097152]{0:T(1024)(128)(4,1)S(1)}, s32[]{:S(2)}) async-start(s8[10485760]{0:T(1024)(128)(4,1)} %bitcast.98), calls=%async_computation.2 | async-start | bytes 4194304
where the time goes:
time: 244 us
  other arithmetic  95 us (39%)
  local copies, waits for them, and re-layouts  88.2 us (36%)
  waiting for transfers between devices  45.6 us (19%)
  starting transfers between devices  14.9 us (6%)
    add x2, other arithmetic, advance_flat(): weights[0] * middle + weights[1] * western + weights[2] * eastern  45.2 us
    slice x3, local copies, waits for them, and re-layouts, substep(): jnp.roll(middle, -1, axis=1)  30.3 us
    add x2, other arithmetic, substep(): weights[0] * middle + weights[1] * jnp.roll(middle, 1, axis=1)  28.1 us
    ppermute x2, waiting for transfers between devices, extended(): before = lax.ppermute(last, axis, up)  27.4 us
    slice x4, local copies, waits for them, and re-layouts, advance_flat(): jnp.roll(middle, -1, axis=1)  22.7 us
    slice x4, local copies, waits for them, and re-layouts, advance_flat(): jnp.roll(middle, nlon - 1, axis=1)  20.6 us
    ppermute x2, waiting for transfers between devices, extended(): after = lax.ppermute(first, axis, down)  18.2 us
    concatenate x2, other arithmetic, extended(): array = jnp.concatenate([before, array, after], axis=dim)  14.7 us
  transfers between devices with their start and end apart: 4, of which 4 were waited for; matrix products, arithmetic and copies ran while one was open for 4% of the time, Pallas kernels for 0%

commit v1 on v0

v1 whole, which is shorter than its diff:
```python
import functools

import jax
import jax.numpy as jnp
from jax import lax
from jax.experimental import pallas as pl
from jax.experimental.pallas import tpu as pltpu
from jax.sharding import PartitionSpec as P

NLAT = 128
NLON = 128
CLASSES = 8
MESH = pl.DeviceIdType.MESH
HALO = 2 * NLON

X_CHUNKS = ((0, 2), (14, 2), (2, 4), (6, 4), (10, 2), (12, 2))
COL_ROWS = 32
ROW_BLOCK = 32


def lookup(codes, tab_ref, line):
    value = jnp.full(codes.shape, tab_ref[line, 0], jnp.float32)
    for cls in range(1, CLASSES):
        value = jnp.where(codes == cls, tab_ref[line, cls], value)
    return value


def weights_of(lat, wd_ref, ws_ref, tab_ref, dif_ref):
    inside = jnp.logical_and(lat >= 0, lat < NLAT)
    lat = jnp.clip(lat, 0, NLAT - 1)
    spot = pl.ds(pl.multiple_of(lat * NLON, NLON), NLON)
    direction = wd_ref[:, spot]
    speed = ws_ref[:, spot]
    u = lookup(speed, tab_ref, 0)
    v = lookup(speed, tab_ref, 1)
    e = jnp.where((direction & 1) == 0, 1.0, 0.0)
    n = jnp.where(direction < 2, 1.0, 0.0)
    k = dif_ref[lat]
    keep = jnp.where(inside, 1.0, 0.0)
    return [
        w * keep
        for w in (
            1.0 - u - v - 4.0 * k,
            u * e + k,
            u * (1.0 - e) + k,
            v * n + k,
            v * (1.0 - n) + k,
        )
    ]


def kernel(
    n_rows, n_cols, lat_r, lat_c,
    cov, wd_ref, ws_ref, tab_ref, dif_ref, out,
    X, B, CW, RW, G, lsem, xs, xr, zs, zr,
):
    r = lax.axis_index("row")
    c = lax.axis_index("col")
    left, right, up, down = c > 0, c < n_cols - 1, r > 0, r < n_rows - 1
    rows, cols = lat_r * NLON, lat_c * NLON
    at_left, at_right = {"row": r, "col": c - 1}, {"row": r, "col": c + 1}
    at_up, at_down = {"row": r - 1, "col": c}, {"row": r + 1, "col": c}

    own = [(0, HALO), (rows - HALO, HALO), (HALO, rows - 2 * HALO)]

    def own_copy(i):
        start, size = own[i]
        return pltpu.make_async_copy(
            cov.at[pl.ds(start, size), :], X.at[pl.ds(start, size), pl.ds(HALO, cols)], lsem.at[i]
        )

    barrier = pltpu.get_barrier_semaphore()
    sides = ((left, at_left), (right, at_right), (up, at_up), (down, at_down))
    for have, where in sides:
        @pl.when(have)
        def _():
            pl.semaphore_signal(barrier, inc=1, device_id=where, device_id_type=MESH)
    for i in range(3):
        own_copy(i).start()
    pl.semaphore_wait(barrier, sum(jnp.where(have, 1, 0) for have, _ in sides))

    def x_copy(i, side):
        lat, count = X_CHUNKS[i]
        span = pl.ds(lat * NLON, count * NLON)
        if side == 0:
            src, dst, where = cov.at[span, pl.ds(cols - HALO, HALO)], X.at[span, pl.ds(0, HALO)], at_right
        else:
            src, dst, where = cov.at[span, pl.ds(0, HALO)], X.at[span, pl.ds(HALO + cols, HALO)], at_left
        return pltpu.make_async_remote_copy(
            src_ref=src, dst_ref=dst, send_sem=xs.at[side, i], recv_sem=xr.at[side, i],
            device_id=where, device_id_type=MESH,
        )

    for i in range(len(X_CHUNKS)):
        @pl.when(right)
        def _():
            x_copy(i, 0).start()

        @pl.when(left)
        def _():
            x_copy(i, 1).start()

    Z_PIECES = ((2, 2), (4, 2), (0, 2), (6, 2))

    def z_copy(i, side):
        lat, count = Z_PIECES[i]
        span = pl.ds(lat * NLON, count * NLON)
        if side == 0:
            src, dst, where = B.at[pl.ds(rows, HALO), span], B.at[pl.ds(0, HALO), span], at_down
        else:
            src, dst, where = B.at[pl.ds(HALO, HALO), span], B.at[pl.ds(HALO + rows, HALO), span], at_up
        return pltpu.make_async_remote_copy(
            src_ref=src, dst_ref=dst, send_sem=zs.at[side, i], recv_sem=zr.at[side, i],
            device_id=where, device_id_type=MESH,
        )

    def z_start(i, side):
        @pl.when(down if side == 0 else up)
        def _():
            z_copy(i, side).start()

    def z_wait(i, side):
        @pl.when(up if side == 0 else down)
        def _():
            z_copy(i, side).wait_recv()

    def x_wait(i):
        @pl.when(left)
        def _():
            x_copy(i, 0).wait_recv()

        @pl.when(right)
        def _():
            x_copy(i, 1).wait_recv()

    @pl.when(jnp.logical_not(left))
    def _():
        X[:, pl.ds(0, HALO)] = jnp.zeros((rows, HALO), jnp.float32)

    @pl.when(jnp.logical_not(right))
    def _():
        X[:, pl.ds(HALO + cols, HALO)] = jnp.zeros((rows, HALO), jnp.float32)

    @pl.when(jnp.logical_not(up))
    def _():
        B[pl.ds(0, HALO), :] = jnp.zeros((HALO, cols), jnp.float32)

    @pl.when(jnp.logical_not(down))
    def _():
        B[pl.ds(HALO + rows, HALO), :] = jnp.zeros((HALO, cols), jnp.float32)

    def col_table(i, carry):
        for k, w in enumerate(weights_of(c * lat_c + i - 1, wd_ref, ws_ref, tab_ref, dif_ref)):
            for s in range(2):
                CW[s * 5 + k, i] = jnp.broadcast_to(w[s : s + 1], (8, NLON))
        return carry

    lax.fori_loop(0, lat_c + 2, col_table, 0)

    def stencil(f, west, east, south, north, w):
        return w[0] * f + w[1] * west + w[2] * east + w[3] * south + w[4] * north

    def column_operator(start, count, lo, hi):
        tiles = COL_ROWS // 8

        def lane_step(field, l, s):
            f = field[l]
            w = [CW[s * 5 + k, l + 1][None] for k in range(5)]
            return stencil(f, pltpu.roll(f, 1, 2), pltpu.roll(f, NLON - 1, 2), field[l - 1], field[l + 1], w)

        def body(i, carry):
            at = pl.multiple_of(start + i * COL_ROWS, COL_ROWS)
            f, g = {}, {}

            def fetch(l):
                f[l] = X[pl.ds(at, COL_ROWS), pl.ds(HALO + l * NLON, NLON)].reshape(tiles, 8, NLON)

            fetch(lo - 2)
            fetch(lo - 1)
            for l in range(lo - 1, hi + 1):
                fetch(l + 1)
                g[l] = lane_step(f, l, 0)
                if l - 1 >= lo:
                    o = lane_step(g, l - 1, 1)
                    B[pl.ds(HALO + at, COL_ROWS), pl.ds((l - 1) * NLON, NLON)] = o.reshape(COL_ROWS, NLON)
            return carry

        lax.fori_loop(0, count // COL_ROWS, body, 0)

    def row_step(src, base, span, s, lat, store):
        above, below = base - NLON, base + NLON
        for b in range(NLON // ROW_BLOCK):
            o = b * ROW_BLOCK
            prev, nxt = (o - 8) % NLON, (o + ROW_BLOCK) % NLON
            f = src[pl.ds(base + o, ROW_BLOCK), span]
            wide = jnp.concatenate([src[pl.ds(base + prev, 8), span], f, src[pl.ds(base + nxt, 8), span]], axis=0)
            west = pltpu.roll(wide, 1, 0)[8 : 8 + ROW_BLOCK]
            east = pltpu.roll(wide, ROW_BLOCK + 15, 0)[8 : 8 + ROW_BLOCK]
            w = []
            for k in range(5):
                t = RW[s * 5 + k, lat + 1, pl.ds(o, ROW_BLOCK), :]
                w.append(jnp.concatenate([t, t], axis=1))
            south = src[pl.ds(above + o, ROW_BLOCK), span]
            north = src[pl.ds(below + o, ROW_BLOCK), span]
            store(o, stencil(f, west, east, south, north, w))

    def row_operator(lat0, count, pairs):
        first, n, stride = pairs

        def pair(p, carry):
            span = pl.ds(pl.multiple_of((first + p * stride) * HALO, HALO), HALO)

            def one(i, inner):
                lat = lat0 - 1 + i

                def store(o, value):
                    G[pl.ds(pl.multiple_of(i * NLON, NLON) + o, ROW_BLOCK), :] = value

                row_step(B, pl.multiple_of(HALO + lat * NLON, NLON), span, 0, lat, store)
                return inner

            lax.fori_loop(0, count + 2, one, 0)

            def two(i, inner):
                lat = lat0 + i

                def store(o, value):
                    out[pl.ds(pl.multiple_of(lat * NLON, NLON) + o, ROW_BLOCK), span] = value

                row_step(G, pl.multiple_of((i + 1) * NLON, NLON), slice(None), 1, lat, store)
                return inner

            lax.fori_loop(0, count, two, 0)
            return carry

        lax.fori_loop(0, n, pair, 0)

    INNER, OUTER = (1, 2, 1), (0, 2, 3)
    last = lat_c - 2

    own_copy(1).wait()
    column_operator(rows - HALO, HALO, 2, last)
    for i in range(2):
        z_start(i, 0)
    own_copy(0).wait()
    column_operator(0, HALO, 2, last)
    for i in range(2):
        z_start(i, 1)

    own_copy(2).wait()
    column_operator(HALO, rows - 2 * HALO, 2, last)

    def row_table(i, carry):
        lines = []
        ws = weights_of(r * lat_r + i - 1, wd_ref, ws_ref, tab_ref, dif_ref)
        for s in range(2):
            lines += [w[s : s + 1] for w in ws]
        block = jnp.concatenate(lines + [jnp.zeros((6, NLON), jnp.float32)], axis=0)
        turned = block.T
        for q in range(10):
            RW[q, i] = jnp.broadcast_to(turned[:, q : q + 1], (NLON, NLON))
        return carry

    lax.fori_loop(0, lat_r + 2, row_table, 0)

    def edges(i):
        lat, count = X_CHUNKS[i]
        x_wait(i)
        column_operator(lat * NLON, count * NLON, 0, 2)
        column_operator(lat * NLON, count * NLON, last, lat_c)

    edges(1)
    for i in (2, 3):
        z_start(i, 0)
    edges(0)
    for i in (2, 3):
        z_start(i, 1)

    row_operator(2, lat_r - 4, INNER)
    edges(2)
    row_operator(2, 2, OUTER)
    for i in (0, 1):
        z_wait(i, 0)
        z_wait(i, 1)
    row_operator(0, 2, INNER)
    row_operator(lat_r - 2, 2, INNER)
    edges(3)
    row_operator(4, 4, OUTER)
    edges(4)
    row_operator(8, 2, OUTER)
    edges(5)
    row_operator(10, 4, OUTER)
    for i in (2, 3):
        z_wait(i, 0)
        z_wait(i, 1)
    row_operator(0, 2, OUTER)
    row_operator(lat_r - 2, 2, OUTER)

    for i in range(len(X_CHUNKS)):
        @pl.when(right)
        def _():
            x_copy(i, 0).wait_send()

        @pl.when(left)
        def _():
            x_copy(i, 1).wait_send()
    for i in range(len(Z_PIECES)):
        @pl.when(down)
        def _():
            z_copy(i, 0).wait_send()

        @pl.when(up)
        def _():
            z_copy(i, 1).wait_send()


def solution(mesh):
    n_rows, n_cols = mesh.shape["row"], mesh.shape["col"]
    lat_r, lat_c = NLAT // n_rows, NLAT // n_cols

    def local(cov, wd, ws, tab, dif):
        rows, cols = cov.shape
        vmem = pl.BlockSpec(memory_space=pltpu.VMEM)
        smem = pl.BlockSpec(memory_space=pltpu.SMEM)
        f32 = jnp.float32
        return pl.pallas_call(
            functools.partial(kernel, n_rows, n_cols, lat_r, lat_c),
            out_shape=pltpu.VMEM((rows, cols), f32),
            in_specs=[pl.BlockSpec(memory_space=pl.ANY), vmem, vmem, smem, smem],
            out_specs=vmem,
            scratch_shapes=[
                pltpu.VMEM((rows, cols + 2 * HALO), f32),
                pltpu.VMEM((rows + 2 * HALO, cols), f32),
                pltpu.VMEM((10, lat_c + 2, 8, NLON), f32),
                pltpu.VMEM((10, lat_r + 2, NLON, NLON), f32),
                pltpu.VMEM(((lat_r - 2) * NLON, HALO), f32),
                pltpu.SemaphoreType.DMA((3,)),
                pltpu.SemaphoreType.DMA((2, len(X_CHUNKS))),
                pltpu.SemaphoreType.DMA((2, len(X_CHUNKS))),
                pltpu.SemaphoreType.DMA((2, 4)),
                pltpu.SemaphoreType.DMA((2, 4)),
            ],
            compiler_params=pltpu.CompilerParams(
                collective_id=0, has_side_effects=True, vmem_limit_bytes=50 << 20
            ),
        )(cov, wd, ws, tab, dif)

    return jax.shard_map(
        local,
        mesh=mesh,
        in_specs=(P("row", "col"), P(), P(), P(), P()),
        out_specs=P("row", "col"),
        check_vma=False,
    )
```

time: 244 us -> 65.9 us (0.27)
  the two profiles are of different devices: /device:TPU:23 before, /device:TPU:96 now
where the time goes in v1:
time: 65.9 us; the launch traced here: 65.6 us
  Pallas kernels  62.2 us (94%)
  local copies, waits for them, and re-layouts  3.4 us (5%)
    pallas_call x1, Pallas kernels, local(): pl.pallas_call(functools.partial(kernel, n_rows, n_cols, lat_r, lat_c), o...  62.2 us
    unnamed x1, local copies, waits for them, and re-layouts  3.4 us

profile of v1, /device:TPU:96, one launch (start us, length us, event | category | flops | bytes accessed | tf_op | source)
XLA Modules:
  0.0 65.6 jit_solution(8145342426884246795)
XLA Ops:
  0.0 62.2 %shard_map.55 = f32[2048,1024]{1,0:T(8,128)S(1)} custom-call(f32[2048,1024]{1,0:T(8,128)} %cov.1, s32[2,16384]{1,0:T(2,128)} %wd_ref.1, s32[2,16384]{1,0:T(2,128)} %ws_ref.1, f32[2,8]{1,0:T(2,128)} %tab_ref.1, f32[128]{0:T(128)} %dif_ref.1), custom_call_target="tpu_custom_call" | custom-call | tf_op jit(solution)/shard_map/pallas_call | solution.py:326
  62.2 3.4 %copy.7 = f32[2048,1024]{1,0:T(8,128)} copy(f32[2048,1024]{1,0:T(8,128)S(1)} %shard_map.55) | data formatting | bytes 16777216

commit v2 on v1

v2 whole, which is shorter than its diff:
```python
import functools

import jax
import jax.numpy as jnp
from jax import lax
from jax.experimental import pallas as pl
from jax.experimental.pallas import tpu as pltpu
from jax.sharding import PartitionSpec as P

NLAT = 128
NLON = 128
CLASSES = 8
MESH = pl.DeviceIdType.MESH
HALO = 2 * NLON
PAD = 8

X_CHUNKS = ((14, 2), (0, 2), (2, 4), (6, 4), (10, 2), (12, 2))
X_RELAYED = (2, 3)
Z_PIECES = ((2, 2), (4, 2), (0, 2), (6, 2))
Z_RELAYED = (1, 3)
ROW_BLOCK = 32


def lookup(codes, tab_ref, line):
    value = jnp.full(codes.shape, tab_ref[line, 0], jnp.float32)
    for cls in range(1, CLASSES):
        value = jnp.where(codes == cls, tab_ref[line, cls], value)
    return value


def weights_of(lat, wd_ref, ws_ref, tab_ref, dif_ref):
    inside = jnp.logical_and(lat >= 0, lat < NLAT)
    lat = jnp.clip(lat, 0, NLAT - 1)
    spot = pl.ds(pl.multiple_of(lat * NLON, NLON), NLON)
    direction = wd_ref[:, spot]
    speed = ws_ref[:, spot]
    u = lookup(speed, tab_ref, 0)
    v = lookup(speed, tab_ref, 1)
    e = jnp.where((direction & 1) == 0, 1.0, 0.0)
    n = jnp.where(direction < 2, 1.0, 0.0)
    k = dif_ref[lat]
    keep = jnp.where(inside, 1.0, 0.0)
    return [
        w * keep
        for w in (
            1.0 - u - v - 4.0 * k,
            u * e + k,
            u * (1.0 - e) + k,
            v * n + k,
            v * (1.0 - n) + k,
        )
    ]


def kernel(
    n_rows, n_cols, lat_r, lat_c,
    cov, wd_ref, ws_ref, tab_ref, dif_ref, out,
    X, B, CW, RW, G, RX, RZ,
    lsem, xs, xr, zs, zr, rxs, rxr, rzs, rzr,
):
    r = lax.axis_index("row")
    c = lax.axis_index("col")
    left, right, up, down = c > 0, c < n_cols - 1, r > 0, r < n_rows - 1
    rows, cols = lat_r * NLON, lat_c * NLON

    def at(row, col):
        return {"row": row, "col": col}

    mid_r, mid_c = n_rows // 2, n_cols // 2
    q = lax.rem(c, mid_c)
    z_cross = jnp.logical_or(q < 2, q >= mid_c - 2)
    p = lax.rem(r, mid_r)
    x_cross = jnp.logical_or(p == 0, p == mid_r - 1)

    def z_role(row):
        return jnp.logical_and(z_cross, r == row)

    def x_role(col):
        return jnp.logical_and(x_cross, c == col)

    end_r, end_c = n_rows - 1, n_cols - 1
    peers = [(left, at(r, c - 1)), (right, at(r, c + 1)), (up, at(r - 1, c)), (down, at(r + 1, c))]
    for a, b in ((mid_r - 1, 0), (0, mid_r), (mid_r, end_r), (end_r, mid_r - 1)):
        peers += [(z_role(a), at(b, c)), (z_role(b), at(a, c))]
    for a, b in ((mid_c - 1, end_c), (end_c, mid_c), (mid_c, 0), (0, mid_c - 1)):
        peers += [(x_role(a), at(r, b)), (x_role(b), at(r, a))]

    own = [(rows - HALO, HALO), (0, HALO), (HALO, rows - 2 * HALO)]

    def own_copy(i):
        start, size = own[i]
        return pltpu.make_async_copy(
            cov.at[pl.ds(start, size), :], X.at[pl.ds(start, size), pl.ds(HALO, cols)], lsem.at[i]
        )

    barrier = pltpu.get_barrier_semaphore()
    for have, where in peers:
        @pl.when(have)
        def _():
            pl.semaphore_signal(barrier, inc=1, device_id=where, device_id_type=MESH)
    for i in range(3):
        own_copy(i).start()

    def col_table(i, carry):
        for k, w in enumerate(weights_of(c * lat_c + i - 1, wd_ref, ws_ref, tab_ref, dif_ref)):
            for s in range(2):
                CW[s * 5 + k, i] = jnp.broadcast_to(w[s : s + 1], (8, NLON))
        return carry

    lax.fori_loop(0, lat_c + 2, col_table, 0)

    pl.semaphore_wait(barrier, sum(jnp.where(have, 1, 0) for have, _ in peers))

    def remote(src, dst, send, recv, where):
        return lambda: pltpu.make_async_remote_copy(
            src_ref=src, dst_ref=dst, send_sem=send, recv_sem=recv, device_id=where, device_id_type=MESH
        )

    def x_halo(i, side):
        lat, count = X_CHUNKS[i]
        return X.at[pl.ds(lat * NLON, count * NLON), pl.ds(0 if side == 0 else HALO + cols, HALO)]

    def x_copies(i, side):
        lat, count = X_CHUNKS[i]
        src = cov.at[pl.ds(lat * NLON, count * NLON), pl.ds(cols - HALO if side == 0 else 0, HALO)]
        have, where = (right, at(r, c + 1)) if side == 0 else (left, at(r, c - 1))
        direct = remote(src, x_halo(i, side), xs.at[side, i], xr.at[side, i], where)
        if i not in X_RELAYED:
            return [(have, direct)]
        slot = X_RELAYED.index(i)
        source, relay = (mid_c - 1, end_c) if side == 0 else (mid_c, 0)
        by_relay = remote(src, RX.at[slot], xs.at[side, i], rxr.at[slot], at(r, relay))
        here = x_role(source)
        return [(jnp.logical_and(have, jnp.logical_not(here)), direct), (here, by_relay)]

    def x_forwards(slot):
        i = X_RELAYED[slot]
        return [
            (x_role(end_c), remote(RX.at[slot], x_halo(i, 0), rxs.at[slot], xr.at[0, i], at(r, mid_c))),
            (x_role(0), remote(RX.at[slot], x_halo(i, 1), rxs.at[slot], xr.at[1, i], at(r, mid_c - 1))),
        ]

    def z_halo(i, side):
        lat, count = Z_PIECES[i]
        return B.at[pl.ds(lat, count), pl.ds(0 if side == 0 else lat_r + 2, 2), pl.ds(PAD, NLON), :]

    def z_copies(i, side):
        lat, count = Z_PIECES[i]
        src = B.at[pl.ds(lat, count), pl.ds(lat_r if side == 0 else 2, 2), pl.ds(PAD, NLON), :]
        have, where = (down, at(r + 1, c)) if side == 0 else (up, at(r - 1, c))
        direct = remote(src, z_halo(i, side), zs.at[side, i], zr.at[side, i], where)
        if i not in Z_RELAYED:
            return [(have, direct)]
        slot = Z_RELAYED.index(i)
        source, relay = (mid_r - 1, 0) if side == 0 else (mid_r, end_r)
        by_relay = remote(src, RZ.at[slot], zs.at[side, i], rzr.at[slot], at(relay, c))
        here = z_role(source)
        return [(jnp.logical_and(have, jnp.logical_not(here)), direct), (here, by_relay)]

    def z_forwards(slot):
        i = Z_RELAYED[slot]
        return [
            (z_role(0), remote(RZ.at[slot], z_halo(i, 0), rzs.at[slot], zr.at[0, i], at(mid_r, c))),
            (z_role(end_r), remote(RZ.at[slot], z_halo(i, 1), rzs.at[slot], zr.at[1, i], at(mid_r - 1, c))),
        ]

    def start(copies):
        for have, copy in copies:
            @pl.when(have)
            def _():
                copy().start()

    def wait_sent(copies):
        for have, copy in copies:
            @pl.when(have)
            def _():
                copy().wait_send()

    def x_forward(slot):
        @pl.when(jnp.logical_or(x_role(0), x_role(end_c)))
        def _():
            x_copies(X_RELAYED[slot], 0)[1][1]().wait_recv()

        start(x_forwards(slot))

    def z_forward(slot):
        @pl.when(jnp.logical_or(z_role(0), z_role(end_r)))
        def _():
            z_copies(Z_RELAYED[slot], 0)[1][1]().wait_recv()

        start(z_forwards(slot))

    def z_start(i, side):
        start(z_copies(i, side))

    def z_wait(i):
        lat, count = Z_PIECES[i]
        for side, have in ((0, up), (1, down)):
            @pl.when(have)
            def _():
                z_copies(i, side)[0][1]().wait_recv()

            for a in (0, 1):
                y = a + (0 if side == 0 else lat_r + 2)
                for l in range(lat, lat + count):
                    B[l, y, pl.ds(0, PAD), :] = B[l, y, pl.ds(NLON, PAD), :]
                    B[l, y, pl.ds(PAD + NLON, PAD), :] = B[l, y, pl.ds(PAD, PAD), :]

    def x_wait(i):
        for side, have in ((0, left), (1, right)):
            @pl.when(have)
            def _():
                x_copies(i, side)[0][1]().wait_recv()

    for i in range(len(X_CHUNKS)):
        for side in (0, 1):
            start(x_copies(i, side))

    def stencil(f, west, east, south, north, w):
        return w[0] * f + w[1] * west + w[2] * east + w[3] * south + w[4] * north

    tiles = NLON // 8

    def column_operator(lat0, count, spans):
        def lane_step(field, l, s):
            f = field[l]
            w = [CW[s * 5 + k, l + 1][None] for k in range(5)]
            return stencil(f, pltpu.roll(f, 1, 2), pltpu.roll(f, NLON - 1, 2), field[l - 1], field[l + 1], w)

        def body(i, carry):
            y = lat0 + i
            here = pl.ds(pl.multiple_of(y * NLON, NLON), NLON)
            for lo, hi in spans:
                f, g = {}, {}
                for l in range(lo - 2, hi + 2):
                    f[l] = X[here, pl.ds(HALO + l * NLON, NLON)].reshape(tiles, 8, NLON)
                    if l > lo - 1:
                        g[l - 1] = lane_step(f, l - 1, 0)
                    if l > lo + 1:
                        o = lane_step(g, l - 2, 1)
                        B[l - 2, y + 2, pl.ds(PAD, NLON), :] = o.reshape(NLON, NLON)
                        B[l - 2, y + 2, pl.ds(0, PAD), :] = o[tiles - 1]
                        B[l - 2, y + 2, pl.ds(PAD + NLON, PAD), :] = o[0]
            return carry

        lax.fori_loop(0, count, body, 0)

    def row_step(src, first, y, s, lat, store):
        for b in range(NLON // ROW_BLOCK):
            o = b * ROW_BLOCK
            w = [RW[s * 5 + k, lat + 1, pl.ds(o, ROW_BLOCK), :] for k in range(5)]
            for l in (0, 1):
                near = [src[first + l, y, pl.ds(PAD + o + d, ROW_BLOCK), :] for d in (0, -1, 1)]
                south = src[first + l, y - 1, pl.ds(PAD + o, ROW_BLOCK), :]
                north = src[first + l, y + 1, pl.ds(PAD + o, ROW_BLOCK), :]
                store(l, o, stencil(*near, south, north, w))

    def row_operator(lat0, count, pairs):
        first, n, stride = pairs

        def pair(j, carry):
            l0 = (first + j * stride) * 2
            span = [pl.ds(pl.multiple_of((l0 + l) * NLON, NLON), NLON) for l in (0, 1)]

            def one(i, inner):
                lat = lat0 - 1 + i

                def store(l, o, value):
                    G[l, i, pl.ds(PAD + o, ROW_BLOCK), :] = value
                    if o == 0:
                        G[l, i, pl.ds(PAD + NLON, PAD), :] = value[:PAD]
                    if o == NLON - ROW_BLOCK:
                        G[l, i, pl.ds(0, PAD), :] = value[ROW_BLOCK - PAD :]

                row_step(B, l0, lat + 2, 0, lat, store)
                return inner

            lax.fori_loop(0, count + 2, one, 0, unroll=2)

            def two(i, inner):
                lat = lat0 + i
                base = pl.multiple_of(lat * NLON, NLON)

                def store(l, o, value):
                    out[pl.ds(base + o, ROW_BLOCK), span[l]] = value

                row_step(G, 0, i + 1, 1, lat, store)
                return inner

            lax.fori_loop(0, count, two, 0, unroll=2)
            return carry

        lax.fori_loop(0, n, pair, 0)

    INNER, OUTER = (1, 2, 1), (0, 2, 3)
    inner, outer = ((2, lat_c - 2),), ((0, 2), (lat_c - 2, lat_c))

    own_copy(0).wait()
    column_operator(lat_r - 2, 2, inner)
    for i in (0, 1):
        z_start(i, 0)
    own_copy(1).wait()
    column_operator(0, 2, inner)
    for i in (0, 1):
        z_start(i, 1)

    own_copy(2).wait()
    column_operator(2, lat_r - 4, inner)

    @pl.when(jnp.logical_not(left))
    def _():
        X[:, pl.ds(0, HALO)] = jnp.zeros((rows, HALO), jnp.float32)

    @pl.when(jnp.logical_not(right))
    def _():
        X[:, pl.ds(HALO + cols, HALO)] = jnp.zeros((rows, HALO), jnp.float32)

    @pl.when(jnp.logical_not(up))
    def _():
        B[:, pl.ds(0, 2)] = jnp.zeros((lat_c, 2, NLON + 2 * PAD, NLON), jnp.float32)

    @pl.when(jnp.logical_not(down))
    def _():
        B[:, pl.ds(lat_r + 2, 2)] = jnp.zeros((lat_c, 2, NLON + 2 * PAD, NLON), jnp.float32)

    def edges(i):
        x_wait(i)
        column_operator(*X_CHUNKS[i], outer)

    edges(0)
    for i in (2, 3):
        z_start(i, 0)
    edges(1)
    for i in (2, 3):
        z_start(i, 1)
    x_forward(0)
    z_forward(0)

    def row_table(i, carry):
        lat = jnp.clip(r * lat_r + i - 1, 0, NLAT - 1)
        spot = pl.ds(pl.multiple_of(lat * NLON, NLON), NLON)
        direction, speed = wd_ref[:, spot], ws_ref[:, spot]
        u, v = lookup(speed, tab_ref, 0), lookup(speed, tab_ref, 1)
        u = jnp.where((direction & 1) == 0, u, -u)
        v = jnp.where(direction < 2, v, -v)
        k = dif_ref[lat]
        turned = jnp.concatenate([u, v, u, v], axis=0).T
        for s in range(2):
            su = jnp.broadcast_to(turned[:, s : s + 1], (NLON, NLON))
            sv = jnp.broadcast_to(turned[:, 2 + s : 3 + s], (NLON, NLON))
            RW[s * 5, i] = 1.0 - jnp.abs(su) - jnp.abs(sv) - 4.0 * k
            RW[s * 5 + 1, i] = jnp.maximum(su, 0.0) + k
            RW[s * 5 + 2, i] = jnp.maximum(-su, 0.0) + k
            RW[s * 5 + 3, i] = jnp.maximum(sv, 0.0) + k
            RW[s * 5 + 4, i] = jnp.maximum(-sv, 0.0) + k
        return carry

    lax.fori_loop(0, lat_r + 2, row_table, 0, unroll=2)

    @pl.when(jnp.logical_not(up))
    def _():
        RW[:, 0] = jnp.zeros((10, NLON, NLON), jnp.float32)

    @pl.when(jnp.logical_not(down))
    def _():
        RW[:, lat_r + 1] = jnp.zeros((10, NLON, NLON), jnp.float32)

    row_operator(2, lat_r - 4, INNER)
    edges(2)
    x_forward(1)
    row_operator(2, 2, OUTER)
    z_wait(0)
    z_wait(1)
    row_operator(0, 2, INNER)
    row_operator(lat_r - 2, 2, INNER)
    edges(3)
    row_operator(4, 4, OUTER)
    z_forward(1)
    edges(4)
    row_operator(8, 2, OUTER)
    edges(5)
    row_operator(10, 4, OUTER)
    z_wait(2)
    z_wait(3)
    row_operator(0, 2, OUTER)
    row_operator(lat_r - 2, 2, OUTER)

    for side in (0, 1):
        for i in range(len(X_CHUNKS)):
            wait_sent(x_copies(i, side))
        for i in range(len(Z_PIECES)):
            wait_sent(z_copies(i, side))
    for slot in (0, 1):
        wait_sent(x_forwards(slot))
        wait_sent(z_forwards(slot))


def solution(mesh):
    n_rows, n_cols = mesh.shape["row"], mesh.shape["col"]
    lat_r, lat_c = NLAT // n_rows, NLAT // n_cols

    def local(cov, wd, ws, tab, dif):
        rows, cols = cov.shape
        vmem = pl.BlockSpec(memory_space=pltpu.VMEM)
        smem = pl.BlockSpec(memory_space=pltpu.SMEM)
        f32 = jnp.float32
        return pl.pallas_call(
            functools.partial(kernel, n_rows, n_cols, lat_r, lat_c),
            out_shape=pltpu.VMEM((rows, cols), f32),
            in_specs=[pl.BlockSpec(memory_space=pl.ANY), vmem, vmem, smem, smem],
            out_specs=vmem,
            scratch_shapes=[
                pltpu.VMEM((rows, cols + 2 * HALO), f32),
                pltpu.VMEM((lat_c, lat_r + 4, NLON + 2 * PAD, NLON), f32),
                pltpu.VMEM((10, lat_c + 2, 8, NLON), f32),
                pltpu.VMEM((10, lat_r + 2, NLON, NLON), f32),
                pltpu.VMEM((2, lat_r - 2, NLON + 2 * PAD, NLON), f32),
                pltpu.VMEM((2, 4 * NLON, HALO), f32),
                pltpu.VMEM((2, 2, 2, NLON, NLON), f32),
                pltpu.SemaphoreType.DMA((3,)),
                pltpu.SemaphoreType.DMA((2, len(X_CHUNKS))),
                pltpu.SemaphoreType.DMA((2, len(X_CHUNKS))),
                pltpu.SemaphoreType.DMA((2, len(Z_PIECES))),
                pltpu.SemaphoreType.DMA((2, len(Z_PIECES))),
                pltpu.SemaphoreType.DMA((2,)),
                pltpu.SemaphoreType.DMA((2,)),
                pltpu.SemaphoreType.DMA((2,)),
                pltpu.SemaphoreType.DMA((2,)),
            ],
            compiler_params=pltpu.CompilerParams(
                collective_id=0, has_side_effects=True, vmem_limit_bytes=52 << 20
            ),
        )(cov, wd, ws, tab, dif)

    return jax.shard_map(
        local,
        mesh=mesh,
        in_specs=(P("row", "col"), P(), P(), P(), P()),
        out_specs=P("row", "col"),
        check_vma=False,
    )
```

time: 65.9 us -> 45.7 us (0.69)
  the two profiles are of different devices: /device:TPU:96 before, /device:TPU:24 now
where the time goes in v2:
time: 45.7 us; the launch traced here: 45.5 us
  Pallas kernels  42.1 us (92%)
  local copies, waits for them, and re-layouts  3.4 us (7%)
    pallas_call x1, Pallas kernels, local(): pl.pallas_call(functools.partial(kernel, n_rows, n_cols, lat_r, lat_c), o...  42.1 us
    unnamed x1, local copies, waits for them, and re-layouts  3.4 us

profile of v2, /device:TPU:24, one launch (start us, length us, event | category | flops | bytes accessed | tf_op | source)
XLA Modules:
  0.0 45.5 jit_solution(4925065408790275795)
XLA Ops:
  0.0 42.1 %shard_map.55 = f32[2048,1024]{1,0:T(8,128)S(1)} custom-call(f32[2048,1024]{1,0:T(8,128)} %cov.1, s32[2,16384]{1,0:T(2,128)} %wd_ref.1, s32[2,16384]{1,0:T(2,128)} %ws_ref.1, f32[2,8]{1,0:T(2,128)} %tab_ref.1, f32[128]{0:T(128)} %dif_ref.1), custom_call_target="tpu_custom_call" | custom-call | tf_op jit(solution)/shard_map/pallas_call | solution.py:407
  42.1 3.4 %copy.7 = f32[2048,1024]{1,0:T(8,128)} copy(f32[2048,1024]{1,0:T(8,128)S(1)} %shard_map.55) | data formatting | bytes 16777216

commit v3 on v2

--- a/solution.py
+++ b/solution.py
@@ -15,9 +15,9 @@
 PAD = 8
 
 X_CHUNKS = ((14, 2), (0, 2), (2, 4), (6, 4), (10, 2), (12, 2))
-X_RELAYED = (2, 3)
+X_RELAYED = (3, 4, 5)
 Z_PIECES = ((2, 2), (4, 2), (0, 2), (6, 2))
-Z_RELAYED = (1, 3)
+Z_RELAYED = (0, 1)
 ROW_BLOCK = 32
 
 
@@ -55,7 +55,7 @@
 def kernel(
     n_rows, n_cols, lat_r, lat_c,
     cov, wd_ref, ws_ref, tab_ref, dif_ref, out,
-    X, B, CW, RW, G, RX, RZ,
+    X, B, CW, RW, G, RX, RZ, SH,
     lsem, xs, xr, zs, zr, rxs, rxr, rzs, rzr,
 ):
     r = lax.axis_index("row")
@@ -101,13 +101,19 @@
     for i in range(3):
         own_copy(i).start()
 
+    src_lon = lax.broadcasted_iota(jnp.int32, (2 * NLON, 2 * NLON), 0) & (NLON - 1)
+    dst = lax.broadcasted_iota(jnp.int32, (2 * NLON, 2 * NLON), 1)
+    step = jnp.where(dst < NLON, 1, NLON - 1)
+    hit = ((src_lon + step) & (NLON - 1)) == (dst & (NLON - 1))
+    SH[...] = jnp.where(hit, 1.0, 0.0).astype(jnp.bfloat16)
+
     def col_table(i, carry):
         for k, w in enumerate(weights_of(c * lat_c + i - 1, wd_ref, ws_ref, tab_ref, dif_ref)):
             for s in range(2):
                 CW[s * 5 + k, i] = jnp.broadcast_to(w[s : s + 1], (8, NLON))
         return carry
 
-    lax.fori_loop(0, lat_c + 2, col_table, 0)
+    lax.fori_loop(0, lat_c + 2, col_table, 0, unroll=2)
 
     pl.semaphore_wait(barrier, sum(jnp.where(have, 1, 0) for have, _ in peers))
 
@@ -119,6 +125,9 @@
     def x_halo(i, side):
         lat, count = X_CHUNKS[i]
         return X.at[pl.ds(lat * NLON, count * NLON), pl.ds(0 if side == 0 else HALO + cols, HALO)]
+
+    def x_stop(slot):
+        return RX.at[slot, pl.ds(0, X_CHUNKS[X_RELAYED[slot]][1] * NLON)]
 
     def x_copies(i, side):
         lat, count = X_CHUNKS[i]
@@ -129,15 +138,15 @@
             return [(have, direct)]
         slot = X_RELAYED.index(i)
         source, relay = (mid_c - 1, end_c) if side == 0 else (mid_c, 0)
-        by_relay = remote(src, RX.at[slot], xs.at[side, i], rxr.at[slot], at(r, relay))
+        by_relay = remote(src, x_stop(slot), xs.at[side, i], rxr.at[slot], at(r, relay))
         here = x_role(source)
         return [(jnp.logical_and(have, jnp.logical_not(here)), direct), (here, by_relay)]
 
     def x_forwards(slot):
         i = X_RELAYED[slot]
         return [
-            (x_role(end_c), remote(RX.at[slot], x_halo(i, 0), rxs.at[slot], xr.at[0, i], at(r, mid_c))),
-            (x_role(0), remote(RX.at[slot], x_halo(i, 1), rxs.at[slot], xr.at[1, i], at(r, mid_c - 1))),
+            (x_role(end_c), remote(x_stop(slot), x_halo(i, 0), rxs.at[slot], xr.at[0, i], at(r, mid_c))),
+            (x_role(0), remote(x_stop(slot), x_halo(i, 1), rxs.at[slot], xr.at[1, i], at(r, mid_c - 1))),
         ]
 
     def z_halo(i, side):
@@ -212,9 +221,16 @@
             def _():
                 x_copies(i, side)[0][1]().wait_recv()
 
-    for i in range(len(X_CHUNKS)):
+    def x_start(i, ways=slice(None)):
         for side in (0, 1):
-            start(x_copies(i, side))
+            start(x_copies(i, side)[ways])
+
+    DIRECT, BY_RELAY = slice(0, 1), slice(1, 2)
+
+    x_start(0)
+    x_start(1)
+    for i in X_RELAYED:
+        x_start(i, BY_RELAY)
 
     def stencil(f, west, east, south, north, w):
         return w[0] * f + w[1] * west + w[2] * east + w[3] * south + w[4] * north
@@ -222,10 +238,21 @@
     tiles = NLON // 8
 
     def column_operator(lat0, count, spans):
+        def shifted(f, by_matrix):
+            if not by_matrix:
+                return pltpu.roll(f, 1, 2), pltpu.roll(f, NLON - 1, 2)
+            flat = f.reshape(NLON, NLON)
+            high = flat.astype(jnp.bfloat16)
+            low = (flat - high.astype(jnp.float32)).astype(jnp.bfloat16)
+            both = jnp.dot(
+                jnp.concatenate([high, low], axis=1), SH[...], preferred_element_type=jnp.float32
+            )
+            return both[:, :NLON].reshape(f.shape), both[:, NLON:].reshape(f.shape)
+
         def lane_step(field, l, s):
             f = field[l]
             w = [CW[s * 5 + k, l + 1][None] for k in range(5)]
-            return stencil(f, pltpu.roll(f, 1, 2), pltpu.roll(f, NLON - 1, 2), field[l - 1], field[l + 1], w)
+            return stencil(f, *shifted(f, s == 0), field[l - 1], field[l + 1], w)
 
         def body(i, carry):
             y = lat0 + i
@@ -243,7 +270,7 @@
                         B[l - 2, y + 2, pl.ds(PAD + NLON, PAD), :] = o[0]
             return carry
 
-        lax.fori_loop(0, count, body, 0)
+        lax.fori_loop(0, count, body, 0, unroll=2)
 
     def row_step(src, first, y, s, lat, store):
         for b in range(NLON // ROW_BLOCK):
@@ -303,38 +330,6 @@
     column_operator(0, 2, inner)
     for i in (0, 1):
         z_start(i, 1)
-
-    own_copy(2).wait()
-    column_operator(2, lat_r - 4, inner)
-
-    @pl.when(jnp.logical_not(left))
-    def _():
-        X[:, pl.ds(0, HALO)] = jnp.zeros((rows, HALO), jnp.float32)
-
-    @pl.when(jnp.logical_not(right))
-    def _():
-        X[:, pl.ds(HALO + cols, HALO)] = jnp.zeros((rows, HALO), jnp.float32)
-
-    @pl.when(jnp.logical_not(up))
-    def _():
-        B[:, pl.ds(0, 2)] = jnp.zeros((lat_c, 2, NLON + 2 * PAD, NLON), jnp.float32)
-
-    @pl.when(jnp.logical_not(down))
-    def _():
-        B[:, pl.ds(lat_r + 2, 2)] = jnp.zeros((lat_c, 2, NLON + 2 * PAD, NLON), jnp.float32)
-
-    def edges(i):
-        x_wait(i)
-        column_operator(*X_CHUNKS[i], outer)
-
-    edges(0)
-    for i in (2, 3):
-        z_start(i, 0)
-    edges(1)
-    for i in (2, 3):
-        z_start(i, 1)
-    x_forward(0)
-    z_forward(0)
 
     def row_table(i, carry):
         lat = jnp.clip(r * lat_r + i - 1, 0, NLAT - 1)
@@ -365,17 +360,53 @@
     def _():
         RW[:, lat_r + 1] = jnp.zeros((10, NLON, NLON), jnp.float32)
 
+    x_start(2)
+
+    own_copy(2).wait()
+    column_operator(10, 4, inner)
+
+    @pl.when(jnp.logical_not(left))
+    def _():
+        X[:, pl.ds(0, HALO)] = jnp.zeros((rows, HALO), jnp.float32)
+
+    @pl.when(jnp.logical_not(right))
+    def _():
+        X[:, pl.ds(HALO + cols, HALO)] = jnp.zeros((rows, HALO), jnp.float32)
+
+    @pl.when(jnp.logical_not(up))
+    def _():
+        B[:, pl.ds(0, 2)] = jnp.zeros((lat_c, 2, NLON + 2 * PAD, NLON), jnp.float32)
+
+    @pl.when(jnp.logical_not(down))
+    def _():
+        B[:, pl.ds(lat_r + 2, 2)] = jnp.zeros((lat_c, 2, NLON + 2 * PAD, NLON), jnp.float32)
+
+    def edges(i):
+        x_wait(i)
+        column_operator(*X_CHUNKS[i], outer)
+
+    x_forward(0)
+    edges(0)
+    for i in (2, 3):
+        z_start(i, 0)
+    edges(1)
+    for i in (2, 3):
+        z_start(i, 1)
+    z_forward(0)
+    x_start(3, DIRECT)
+
+    column_operator(2, 4, inner)
+    x_forward(1)
+    edges(2)
+    x_forward(2)
+    x_start(4, DIRECT)
+    x_start(5, DIRECT)
+    z_forward(1)
+    column_operator(6, 4, inner)
     row_operator(2, lat_r - 4, INNER)
-    edges(2)
-    x_forward(1)
     row_operator(2, 2, OUTER)
-    z_wait(0)
-    z_wait(1)
-    row_operator(0, 2, INNER)
-    row_operator(lat_r - 2, 2, INNER)
     edges(3)
     row_operator(4, 4, OUTER)
-    z_forward(1)
     edges(4)
     row_operator(8, 2, OUTER)
     edges(5)
@@ -384,14 +415,19 @@
     z_wait(3)
     row_operator(0, 2, OUTER)
     row_operator(lat_r - 2, 2, OUTER)
+    z_wait(0)
+    z_wait(1)
+    row_operator(0, 2, INNER)
+    row_operator(lat_r - 2, 2, INNER)
 
     for side in (0, 1):
         for i in range(len(X_CHUNKS)):
             wait_sent(x_copies(i, side))
         for i in range(len(Z_PIECES)):
             wait_sent(z_copies(i, side))
-    for slot in (0, 1):
+    for slot in range(len(X_RELAYED)):
         wait_sent(x_forwards(slot))
+    for slot in range(len(Z_RELAYED)):
         wait_sent(z_forwards(slot))
 
 
@@ -415,17 +451,18 @@
                 pltpu.VMEM((10, lat_c + 2, 8, NLON), f32),
                 pltpu.VMEM((10, lat_r + 2, NLON, NLON), f32),
                 pltpu.VMEM((2, lat_r - 2, NLON + 2 * PAD, NLON), f32),
-                pltpu.VMEM((2, 4 * NLON, HALO), f32),
+                pltpu.VMEM((len(X_RELAYED), 4 * NLON, HALO), f32),
                 pltpu.VMEM((2, 2, 2, NLON, NLON), f32),
+                pltpu.VMEM((2 * NLON, 2 * NLON), jnp.bfloat16),
                 pltpu.SemaphoreType.DMA((3,)),
                 pltpu.SemaphoreType.DMA((2, len(X_CHUNKS))),
                 pltpu.SemaphoreType.DMA((2, len(X_CHUNKS))),
                 pltpu.SemaphoreType.DMA((2, len(Z_PIECES))),
                 pltpu.SemaphoreType.DMA((2, len(Z_PIECES))),
-                pltpu.SemaphoreType.DMA((2,)),
-                pltpu.SemaphoreType.DMA((2,)),
-                pltpu.SemaphoreType.DMA((2,)),
-                pltpu.SemaphoreType.DMA((2,)),
+                pltpu.SemaphoreType.DMA((len(X_RELAYED),)),
+                pltpu.SemaphoreType.DMA((len(X_RELAYED),)),
+                pltpu.SemaphoreType.DMA((len(Z_RELAYED),)),
+                pltpu.SemaphoreType.DMA((len(Z_RELAYED),)),
             ],
             compiler_params=pltpu.CompilerParams(
                 collective_id=0, has_side_effects=True, vmem_limit_bytes=52 << 20

time: 45.7 us -> 40.2 us (0.88)
  the two profiles are of different devices: /device:TPU:24 before, /device:TPU:96 now
where the time goes in v3:
time: 40.2 us; the launch traced here: 40.1 us
  Pallas kernels  36.7 us (91%)
  local copies, waits for them, and re-layouts  3.4 us (8%)
    pallas_call x1, Pallas kernels, local(): pl.pallas_call(functools.partial(kernel, n_rows, n_cols, lat_r, lat_c), o...  36.7 us
    unnamed x1, local copies, waits for them, and re-layouts  3.4 us

profile of v3, /device:TPU:96, one launch (start us, length us, event | category | flops | bytes accessed | tf_op | source)
XLA Modules:
  0.0 40.1 jit_solution(7647567251927099501)
XLA Ops:
  0.0 36.7 %shard_map.55 = f32[2048,1024]{1,0:T(8,128)S(1)} custom-call(f32[2048,1024]{1,0:T(8,128)} %cov.1, s32[2,16384]{1,0:T(2,128)} %wd_ref.1, s32[2,16384]{1,0:T(2,128)} %ws_ref.1, f32[2,8]{1,0:T(2,128)} %tab_ref.1, f32[128]{0:T(128)} %dif_ref.1), custom_call_target="tpu_custom_call" | custom-call | tf_op jit(solution)/shard_map/pallas_call | solution.py:443
  36.7 3.4 %copy.7 = f32[2048,1024]{1,0:T(8,128)} copy(f32[2048,1024]{1,0:T(8,128)S(1)} %shard_map.55) | data formatting | bytes 16777216

commit v4 on v3

--- a/solution.py
+++ b/solution.py
@@ -18,6 +18,7 @@
 X_RELAYED = (3, 4, 5)
 Z_PIECES = ((2, 2), (4, 2), (0, 2), (6, 2))
 Z_RELAYED = (0, 1)
+INNER, OUTER = (1, 2, 1), (0, 2, 3)
 ROW_BLOCK = 32
 
 
@@ -52,11 +53,64 @@
     ]
 
 
+def stencil(f, west, east, south, north, w):
+    return w[0] * f + w[1] * west + w[2] * east + w[3] * south + w[4] * north
+
+
+def row_step(src, RW, first, y, s, lat, store):
+    for b in range(NLON // ROW_BLOCK):
+        o = b * ROW_BLOCK
+        w = [RW[s * 5 + k, lat + 1, pl.ds(o, ROW_BLOCK), :] for k in range(5)]
+        for l in (0, 1):
+            near = [src[first + l, y, pl.ds(PAD + o + d, ROW_BLOCK), :] for d in (0, -1, 1)]
+            south = src[first + l, y - 1, pl.ds(PAD + o, ROW_BLOCK), :]
+            north = src[first + l, y + 1, pl.ds(PAD + o, ROW_BLOCK), :]
+            store(l, o, stencil(*near, south, north, w))
+
+
+def row_operator_into(out, B, RW, G, lat0, count, pairs):
+    first, n, stride = pairs
+
+    def pair(j, carry):
+        l0 = (first + j * stride) * 2
+        span = [pl.ds(pl.multiple_of((l0 + l) * NLON, NLON), NLON) for l in (0, 1)]
+
+        def one(i, inner):
+            lat = lat0 - 1 + i
+
+            def store(l, o, value):
+                G[l, i, pl.ds(PAD + o, ROW_BLOCK), :] = value
+                if o == 0:
+                    G[l, i, pl.ds(PAD + NLON, PAD), :] = value[:PAD]
+                if o == NLON - ROW_BLOCK:
+                    G[l, i, pl.ds(0, PAD), :] = value[ROW_BLOCK - PAD :]
+
+            row_step(B, RW, l0, lat + 2, 0, lat, store)
+            return inner
+
+        lax.fori_loop(0, count + 2, one, 0, unroll=2)
+
+        def two(i, inner):
+            lat = lat0 + i
+            base = pl.multiple_of(lat * NLON, NLON)
+
+            def store(l, o, value):
+                out[pl.ds(base + o, ROW_BLOCK), span[l]] = value
+
+            row_step(G, RW, 0, i + 1, 1, lat, store)
+            return inner
+
+        lax.fori_loop(0, count, two, 0, unroll=2)
+        return carry
+
+    lax.fori_loop(0, n, pair, 0)
+
+
 def kernel(
     n_rows, n_cols, lat_r, lat_c,
-    cov, wd_ref, ws_ref, tab_ref, dif_ref, out,
-    X, B, CW, RW, G, RX, RZ, SH,
-    lsem, xs, xr, zs, zr, rxs, rxr, rzs, rzr,
+    cov, wd_hbm, ws_hbm, tab_hbm, dif_hbm, out, B, RW,
+    X, CW, G, RX, RZ, SH, wd_ref, ws_ref, tab_ref, dif_ref,
+    tsem, lsem, xs, xr, zs, zr, rxs, rxr, rzs, rzr,
 ):
     r = lax.axis_index("row")
     c = lax.axis_index("col")
@@ -93,6 +147,14 @@
             cov.at[pl.ds(start, size), :], X.at[pl.ds(start, size), pl.ds(HALO, cols)], lsem.at[i]
         )
 
+    tables = [
+        pltpu.make_async_copy(src, dst, tsem.at[i])
+        for i, (src, dst) in enumerate(
+            ((wd_hbm, wd_ref), (ws_hbm, ws_ref), (tab_hbm, tab_ref), (dif_hbm, dif_ref))
+        )
+    ]
+    for copy in tables:
+        copy.start()
     barrier = pltpu.get_barrier_semaphore()
     for have, where in peers:
         @pl.when(have)
@@ -106,6 +168,9 @@
     step = jnp.where(dst < NLON, 1, NLON - 1)
     hit = ((src_lon + step) & (NLON - 1)) == (dst & (NLON - 1))
     SH[...] = jnp.where(hit, 1.0, 0.0).astype(jnp.bfloat16)
+
+    for copy in tables:
+        copy.wait()
 
     def col_table(i, carry):
         for k, w in enumerate(weights_of(c * lat_c + i - 1, wd_ref, ws_ref, tab_ref, dif_ref)):
@@ -231,9 +296,6 @@
     x_start(1)
     for i in X_RELAYED:
         x_start(i, BY_RELAY)
-
-    def stencil(f, west, east, south, north, w):
-        return w[0] * f + w[1] * west + w[2] * east + w[3] * south + w[4] * north
 
     tiles = NLON // 8
 
@@ -272,54 +334,9 @@
 
         lax.fori_loop(0, count, body, 0, unroll=2)
 
-    def row_step(src, first, y, s, lat, store):
-        for b in range(NLON // ROW_BLOCK):
-            o = b * ROW_BLOCK
-            w = [RW[s * 5 + k, lat + 1, pl.ds(o, ROW_BLOCK), :] for k in range(5)]
-            for l in (0, 1):
-                near = [src[first + l, y, pl.ds(PAD + o + d, ROW_BLOCK), :] for d in (0, -1, 1)]
-                south = src[first + l, y - 1, pl.ds(PAD + o, ROW_BLOCK), :]
-                north = src[first + l, y + 1, pl.ds(PAD + o, ROW_BLOCK), :]
-                store(l, o, stencil(*near, south, north, w))
-
     def row_operator(lat0, count, pairs):
-        first, n, stride = pairs
-
-        def pair(j, carry):
-            l0 = (first + j * stride) * 2
-            span = [pl.ds(pl.multiple_of((l0 + l) * NLON, NLON), NLON) for l in (0, 1)]
-
-            def one(i, inner):
-                lat = lat0 - 1 + i
-
-                def store(l, o, value):
-                    G[l, i, pl.ds(PAD + o, ROW_BLOCK), :] = value
-                    if o == 0:
-                        G[l, i, pl.ds(PAD + NLON, PAD), :] = value[:PAD]
-                    if o == NLON - ROW_BLOCK:
-                        G[l, i, pl.ds(0, PAD), :] = value[ROW_BLOCK - PAD :]
-
-                row_step(B, l0, lat + 2, 0, lat, store)
-                return inner
-
-            lax.fori_loop(0, count + 2, one, 0, unroll=2)
-
-            def two(i, inner):
-                lat = lat0 + i
-                base = pl.multiple_of(lat * NLON, NLON)
-
-                def store(l, o, value):
-                    out[pl.ds(base + o, ROW_BLOCK), span[l]] = value
-
-                row_step(G, 0, i + 1, 1, lat, store)
-                return inner
-
-            lax.fori_loop(0, count, two, 0, unroll=2)
-            return carry
-
-        lax.fori_loop(0, n, pair, 0)
-
-    INNER, OUTER = (1, 2, 1), (0, 2, 3)
+        row_operator_into(out, B, RW, G, lat0, count, pairs)
+
     inner, outer = ((2, lat_c - 2),), ((0, 2), (lat_c - 2, lat_c))
 
     own_copy(0).wait()
@@ -411,14 +428,8 @@
     row_operator(8, 2, OUTER)
     edges(5)
     row_operator(10, 4, OUTER)
-    z_wait(2)
-    z_wait(3)
-    row_operator(0, 2, OUTER)
-    row_operator(lat_r - 2, 2, OUTER)
-    z_wait(0)
-    z_wait(1)
-    row_operator(0, 2, INNER)
-    row_operator(lat_r - 2, 2, INNER)
+    for i in (2, 3, 0, 1):
+        z_wait(i)
 
     for side in (0, 1):
         for i in range(len(X_CHUNKS)):
@@ -431,6 +442,24 @@
         wait_sent(z_forwards(slot))
 
 
+def finish(lat_r, out, B, RW, hbm, T, G, sem):
+    def send(src, i, lat, count, first, columns):
+        area = (pl.ds(lat * NLON, count * NLON), pl.ds(first * NLON, columns * NLON))
+        copy = pltpu.make_async_copy(src.at[area], hbm.at[area], sem.at[i])
+        copy.start()
+        return copy
+
+    copies = [send(out, 0, 2, lat_r - 4, 0, 8)]
+    row_operator_into(T, B, RW, G, 0, 2, OUTER)
+    row_operator_into(T, B, RW, G, 0, 2, INNER)
+    copies.append(send(T, 1, 0, 2, 0, 8))
+    row_operator_into(T, B, RW, G, lat_r - 2, 2, OUTER)
+    row_operator_into(T, B, RW, G, lat_r - 2, 2, INNER)
+    copies.append(send(T, 2, lat_r - 2, 2, 0, 8))
+    for copy in copies:
+        copy.wait()
+
+
 def solution(mesh):
     n_rows, n_cols = mesh.shape["row"], mesh.shape["col"]
     lat_r, lat_c = NLAT // n_rows, NLAT // n_cols
@@ -438,22 +467,28 @@
     def local(cov, wd, ws, tab, dif):
         rows, cols = cov.shape
         vmem = pl.BlockSpec(memory_space=pltpu.VMEM)
-        smem = pl.BlockSpec(memory_space=pltpu.SMEM)
         f32 = jnp.float32
-        return pl.pallas_call(
+        out, B, RW = pl.pallas_call(
             functools.partial(kernel, n_rows, n_cols, lat_r, lat_c),
-            out_shape=pltpu.VMEM((rows, cols), f32),
-            in_specs=[pl.BlockSpec(memory_space=pl.ANY), vmem, vmem, smem, smem],
-            out_specs=vmem,
+            out_shape=[
+                pltpu.VMEM((rows, cols), f32),
+                pltpu.VMEM((lat_c, lat_r + 4, NLON + 2 * PAD, NLON), f32),
+                pltpu.VMEM((10, lat_r + 2, NLON, NLON), f32),
+            ],
+            in_specs=[pl.BlockSpec(memory_space=pltpu.MemorySpace.HBM)] * 5,
+            out_specs=[vmem] * 3,
             scratch_shapes=[
                 pltpu.VMEM((rows, cols + 2 * HALO), f32),
-                pltpu.VMEM((lat_c, lat_r + 4, NLON + 2 * PAD, NLON), f32),
                 pltpu.VMEM((10, lat_c + 2, 8, NLON), f32),
-                pltpu.VMEM((10, lat_r + 2, NLON, NLON), f32),
                 pltpu.VMEM((2, lat_r - 2, NLON + 2 * PAD, NLON), f32),
                 pltpu.VMEM((len(X_RELAYED), 4 * NLON, HALO), f32),
                 pltpu.VMEM((2, 2, 2, NLON, NLON), f32),
                 pltpu.VMEM((2 * NLON, 2 * NLON), jnp.bfloat16),
+                pltpu.VMEM(wd.shape, jnp.int32),
+                pltpu.VMEM(ws.shape, jnp.int32),
+                pltpu.SMEM(tab.shape, f32),
+                pltpu.SMEM(dif.shape, f32),
+                pltpu.SemaphoreType.DMA((4,)),
                 pltpu.SemaphoreType.DMA((3,)),
                 pltpu.SemaphoreType.DMA((2, len(X_CHUNKS))),
                 pltpu.SemaphoreType.DMA((2, len(X_CHUNKS))),
@@ -465,9 +500,21 @@
                 pltpu.SemaphoreType.DMA((len(Z_RELAYED),)),
             ],
             compiler_params=pltpu.CompilerParams(
-                collective_id=0, has_side_effects=True, vmem_limit_bytes=52 << 20
+                collective_id=0, has_side_effects=True, vmem_limit_bytes=20 << 20
             ),
-        )(cov, wd, ws, tab, dif)
+        )(*(pltpu.with_memory_space_constraint(a, pltpu.MemorySpace.HBM) for a in (cov, wd, ws, tab, dif)))
+        return pl.pallas_call(
+            functools.partial(finish, lat_r),
+            out_shape=jax.ShapeDtypeStruct((rows, cols), f32),
+            in_specs=[vmem] * 3,
+            out_specs=pl.BlockSpec(memory_space=pl.ANY),
+            scratch_shapes=[
+                pltpu.VMEM((rows, cols), f32),
+                pltpu.VMEM((2, 6, NLON + 2 * PAD, NLON), f32),
+                pltpu.SemaphoreType.DMA((6,)),
+            ],
+            compiler_params=pltpu.CompilerParams(vmem_limit_bytes=14 << 20),
+        )(out, B, RW)
 
     return jax.shard_map(
         local,

time: 40.2 us -> 36.6 us (0.910)
  local copies, waits for them, and re-layouts: 3.4 us -> 0 us
    pallas_call x1, Pallas kernels: 36.7 us -> 33.1 us  [local(): pl.pallas_call(functools.partial(kernel, n_rows, n_cols, lat_r, lat_c), o...]
    pallas_call x0 -> x1, Pallas kernels: none -> 3.41 us  [local(): pl.pallas_call(functools.partial(finish, lat_r), out_shape=jax.ShapeDtype...]
    unnamed x1 -> x0, local copies, waits for them, and re-layouts: 3.4 us -> none
where the time goes in v4:
time: 36.6 us; the launch traced here: 36.5 us
  Pallas kernels  36.5 us (100%)
    pallas_call x1, Pallas kernels, local(): pl.pallas_call(functools.partial(kernel, n_rows, n_cols, lat_r, lat_c), o...  33.1 us
    pallas_call x1, Pallas kernels, local(): pl.pallas_call(functools.partial(finish, lat_r), out_shape=jax.ShapeDtype...  3.41 us

profile of v4, /device:TPU:96, one launch (start us, length us, event | category | flops | bytes accessed | tf_op | source)
XLA Modules:
  0.0 36.5 jit_solution(256063405645387034)
XLA Ops:
  0.0 33.1 %shard_map.55 = (f32[2048,1024]{1,0:T(8,128)S(1)}, f32[8,20,144,128]{3,2,1,0:T(8,128)S(1)}, f32[10,18,128,128]{3,2,1,0:T(8,128)S(1)}) custom-call(f32[2048,1024]{1,0:T(8,128)} %cov.1, s32[2,16384]{1,0:T(2,128)} %wd_hbm.1, s32[2,16384]{1,0:T(2,128)} %ws_hbm.1, f32[2,8]{1,0:T(2,128)} %tab_hbm.1, f32[128]{0:T(128)} %dif_hbm.1), custom_call_target="tpu_custom_call" | custom-call | tf_op jit(solution)/shard_map/pallas_call | solution.py:471
  33.1 3.4 %shard_map.56 = f32[2048,1024]{1,0:T(8,128)} custom-call(f32[2048,1024]{1,0:T(8,128)S(1)} %get-tuple-element.8.out, f32[8,20,144,128]{3,2,1,0:T(8,128)S(1)} %get-tuple-element.9.B, f32[10,18,128,128]{3,2,1,0:T(8,128)S(1)} %get-tuple-element.10.RW), custom_call_target="tpu_custom_call" | custom-call | tf_op jit(solution)/shard_map/pallas_call | solution.py:506

commit v5 on v4

--- a/solution.py
+++ b/solution.py
@@ -180,6 +180,22 @@
 
     lax.fori_loop(0, lat_c + 2, col_table, 0, unroll=2)
 
+    @pl.when(jnp.logical_not(left))
+    def _():
+        X[:, pl.ds(0, HALO)] = jnp.zeros((rows, HALO), jnp.float32)
+
+    @pl.when(jnp.logical_not(right))
+    def _():
+        X[:, pl.ds(HALO + cols, HALO)] = jnp.zeros((rows, HALO), jnp.float32)
+
+    @pl.when(jnp.logical_not(up))
+    def _():
+        B[:, pl.ds(0, 2)] = jnp.zeros((lat_c, 2, NLON + 2 * PAD, NLON), jnp.float32)
+
+    @pl.when(jnp.logical_not(down))
+    def _():
+        B[:, pl.ds(lat_r + 2, 2)] = jnp.zeros((lat_c, 2, NLON + 2 * PAD, NLON), jnp.float32)
+
     pl.semaphore_wait(barrier, sum(jnp.where(have, 1, 0) for have, _ in peers))
 
     def remote(src, dst, send, recv, where):
@@ -381,22 +397,6 @@
 
     own_copy(2).wait()
     column_operator(10, 4, inner)
-
-    @pl.when(jnp.logical_not(left))
-    def _():
-        X[:, pl.ds(0, HALO)] = jnp.zeros((rows, HALO), jnp.float32)
-
-    @pl.when(jnp.logical_not(right))
-    def _():
-        X[:, pl.ds(HALO + cols, HALO)] = jnp.zeros((rows, HALO), jnp.float32)
-
-    @pl.when(jnp.logical_not(up))
-    def _():
-        B[:, pl.ds(0, 2)] = jnp.zeros((lat_c, 2, NLON + 2 * PAD, NLON), jnp.float32)
-
-    @pl.when(jnp.logical_not(down))
-    def _():
-        B[:, pl.ds(lat_r + 2, 2)] = jnp.zeros((lat_c, 2, NLON + 2 * PAD, NLON), jnp.float32)
 
     def edges(i):
         x_wait(i)

time: 36.6 us -> 36.6 us (level)
  no operation moved by 1% of the time
where the time goes in v5:
time: 36.6 us; the launch traced here: 36.5 us
  Pallas kernels  36.5 us (100%)
    pallas_call x1, Pallas kernels, local(): pl.pallas_call(functools.partial(kernel, n_rows, n_cols, lat_r, lat_c), o...  33.1 us
    pallas_call x1, Pallas kernels, local(): pl.pallas_call(functools.partial(finish, lat_r), out_shape=jax.ShapeDtype...  3.41 us

profile of v5, /device:TPU:96, one launch (start us, length us, event | category | flops | bytes accessed | tf_op | source)
XLA Modules:
  0.0 36.5 jit_solution(10229105173351435410)
XLA Ops:
  0.0 33.1 %shard_map.55 = (f32[2048,1024]{1,0:T(8,128)S(1)}, f32[8,20,144,128]{3,2,1,0:T(8,128)S(1)}, f32[10,18,128,128]{3,2,1,0:T(8,128)S(1)}) custom-call(f32[2048,1024]{1,0:T(8,128)} %cov.1, s32[2,16384]{1,0:T(2,128)} %wd_hbm.1, s32[2,16384]{1,0:T(2,128)} %ws_hbm.1, f32[2,8]{1,0:T(2,128)} %tab_hbm.1, f32[128]{0:T(128)} %dif_hbm.1), custom_call_target="tpu_custom_call" | custom-call | tf_op jit(solution)/shard_map/pallas_call | solution.py:471
  33.1 3.4 %shard_map.56 = f32[2048,1024]{1,0:T(8,128)} custom-call(f32[2048,1024]{1,0:T(8,128)S(1)} %get-tuple-element.8.out, f32[8,20,144,128]{3,2,1,0:T(8,128)S(1)} %get-tuple-element.9.B, f32[10,18,128,128]{3,2,1,0:T(8,128)S(1)} %get-tuple-element.10.RW), custom_call_target="tpu_custom_call" | custom-call | tf_op jit(solution)/shard_map/pallas_call | solution.py:506
